TPU v7x, 128 devices: a whole 4x4x4 slice. The times are simulated.
128 devices in a mesh: row: 16 (over z_lo, y, core), col: 8 (over x, z_hi).
Axes of the slice: x: 4, y: 4, z: 4 (z_hi: 2, z_lo: 2; z = z_hi * 2 + z_lo), core: 2. Of those that a mesh axis runs over, the one named last changes fastest.
Arguments:
- features: bfloat16 [32768, 128], P(('col', 'row')), may hold values from -6 to 6
- weight: bfloat16 [128, 256], replicated, may hold values from -0.5 to 0.5
- adj_values: bfloat16 [12288, 256, 256], P(('row', 'col')), may hold values from -0.0390625 to 0.0390625
- slot_rows: int32 [12288], P(('row', 'col')), may hold values from 0 to 7, as said below
- slot_cols: int32 [12288], P(('row', 'col')), may hold values from 0 to 15
- slot_live: int32 [128], P(('row', 'col')), may hold values from 13 to 96, as said below
- cotangent: bfloat16 [32768, 256], P(('row', 'col')), may hold values from -6 to 6
Outputs:
- output: bfloat16 [32768, 256], P(('row', 'col'))
- grad_features: bfloat16 [32768, 128], P(('col', 'row'))
- grad_weight: float32 [128, 256], replicated
Inputs may be any that keep to these rules, and one draw needn't show every extreme that they name: Within one device's slots the pairs (slot_rows, slot_cols) are distinct. `slot_live`: some device has all 96 slots live.
All inputs are finite; a program needn't handle non-finite values.
Results may differ from a plain program's by a relative error of at most 0.006.
Values may be sent and summed in bfloat16 or wider, within the bound.
A program may use at most 128 MiB of HBM per device.

v0:
```python
import math
import jax
import jax.numpy as jnp
from jax import lax
from jax.sharding import PartitionSpec as P


def silu_slope(value):
    sig = jax.nn.sigmoid(value)
    return sig * (1.0 + value * (1.0 - sig))


def block_product(adj_values, index_in, index_out, keep, source, count_out, transposed):
    slots, size = (adj_values.shape[0], adj_values.shape[1])
    width = source.shape[2]
    group = math.gcd(slots, 32)
    groups = slots // group

    def step(total, item):
        values, taken, placed, weights = item
        picked = source[taken]
        if transposed:
            product = jnp.einsum("sab,saf->sbf", values, picked, preferred_element_type=jnp.float32)
        else:
            product = jnp.einsum("sab,sbf->saf", values, picked, preferred_element_type=jnp.float32)
        return (total.at[placed].add(product * weights[:, None, None]), None)

    items = (
        adj_values.reshape(groups, group, size, size),
        index_in.reshape(groups, group),
        index_out.reshape(groups, group),
        keep.reshape(groups, group),
    )
    total, _ = lax.scan(step, jnp.zeros((count_out, size, width), jnp.float32), items)
    return total.reshape(count_out * size, width)


def body(features, weight, adj_values, slot_rows, slot_cols, slot_live, cotangent):
    size = adj_values.shape[1]
    slots = adj_values.shape[0]
    width = weight.shape[1]
    own_rows = features.shape[0]
    per_device = own_rows // size
    tile_rows = per_device * lax.axis_size("col")
    tile_cols = per_device * lax.axis_size("row")
    nodes = own_rows * lax.axis_size("row") * lax.axis_size("col")
    keep = (jnp.arange(slots, dtype=jnp.int32) < slot_live[0]).astype(jnp.float32)
    projected = jnp.dot(features, weight, preferred_element_type=jnp.float32).astype(jnp.bfloat16)
    column_rows = lax.all_gather(projected, "row", axis=0, tiled=True)
    column_blocks = column_rows.reshape(tile_cols, size, width)
    partial_value = block_product(
        adj_values, slot_cols, slot_rows, keep, column_blocks, tile_rows, False
    )
    summed = lax.psum_scatter(partial_value, "col", scatter_dimension=0, tiled=True)
    output = jax.nn.silu(summed).astype(jnp.bfloat16)
    grad_summed = (cotangent.astype(jnp.float32) * silu_slope(summed)).astype(jnp.bfloat16)
    grad_range = lax.all_gather(grad_summed, "col", axis=0, tiled=True)
    grad_blocks = grad_range.reshape(tile_rows, size, width)
    back = block_product(adj_values, slot_rows, slot_cols, keep, grad_blocks, tile_cols, True)
    grad_projected = lax.psum_scatter(back, "row", scatter_dimension=0, tiled=True).astype(
        jnp.bfloat16
    )
    grad_features = jnp.dot(grad_projected, weight.T, preferred_element_type=jnp.float32).astype(
        jnp.bfloat16
    )
    local_term = lax.dot_general(
        features, grad_projected, (((0,), (0,)), ((), ())), preferred_element_type=jnp.float32
    )
    grad_weight = lax.psum(local_term, ("row", "col")) / math.sqrt(nodes)
    return (output, grad_features, grad_weight)


def solution(mesh):
    placed = (
        P(("col", "row"), None),
        P(),
        P(("row", "col"), None, None),
        P(("row", "col")),
        P(("row", "col")),
        P(("row", "col")),
        P(("row", "col"), None),
    )
    return jax.shard_map(
        body,
        mesh=mesh,
        in_specs=placed,
        out_specs=(P(("row", "col"), None), P(("col", "row"), None), P()),
        check_vma=False,
    )
```

profile of v0, /device:TPU:1, one launch (start us, length us, event | category | flops | bytes accessed | tf_op | source)
XLA Modules:
  0.0 557.0 jit_solution(4911130216952027264)
XLA Ops:
  7.2 0.0 all-gather.3.cloned.1.call-start
  7.2 0.8 copy-done
  8.0 1.7 convolution_convert_fusion
  9.7 0.0 all-gather.3.cloned.1.call-update
  9.7 0.0 reduce-scatter.3.cloned.1.call-start
  10.4 0.7 reshape.149
  11.1 0.7 reshape.151
  11.9 35.7 %all-gather.3.cloned.1.call-done = bf16[4096,256]{1,0:T(8,128)(2,1)} async-done(((bf16[256,256]{1,0:T(8,128)(2,1)}), bf16[4096,256]{1,0:T(8,128)(2,1)}) %all-gather.3.cloned.1.call-update) | async-done | bytes 2097168 | tf_op jit(solution)/shard_map/all_gather | solution.py:49
  47.6 0.2 broadcast_in_dim.4
  47.8 72.4 %while.20 = (s32[]{:T(128)}, f32[8,256,256]{2,1,0:T(8,128)S(1)}, s32[3,32]{1,0:T(4,128)S(1)}, bf16[3,32,256,256]{3,2,1,0:T(8,128)(2,1)}, s32[3,32]{1,0:T(4,128)S...) while((s32[]{:T(128)}, f32[8,256,256]{2,1,0:T(8,128)S(1)}, s32[3,32]{1,0:T(4,128)S(1)}, ...), condition=%wide.region_2.3_spmd, body=%wide.region_0.2_spmd.sunk | while | flops 1077937408 | bytes 50337628 | solution.py:34
  47.8 4.4 gather_fusion
  52.2 7.9 %broadcast_multiply_fusion.5 = f32[32,256,256]{2,1,0:T(8,128)} fusion(f32[32]{0:T(128)S(1)} %fusion.42, bf16[32,256,256]{2,1,0:T(8,128)(2,1)} %gather_fusion, bf16[3,32,256,256]{3,2,1,0:T(8,128)(2,1)} %get-tuple-element.236, s32[]{:T(128)} %get-tuple-element.225), kind=kOutput, calls=%fused_computation.6.clone.1 | convolution fusion | flops 1075838976 | bytes 16777856 | tf_op jit(solution)/shard_map/while/body/eval_jaxpr/sab,sbf->saf/dot_general | solution.py:25
  60.2 11.8 %scatter_fusion = f32[8,256,256]{2,1,0:T(8,128)S(1)} fusion(f32[8,256,256]{2,1,0:T(8,128)S(1)} %get-tuple-element.226, s32[32]{0:T(128)S(1)} %get-tuple-element.206, f32[32,256,256]{2,1,0:T(8,128)} %broadcast_multiply_fusion.5), kind=kCustom, calls=%fused_computation.2.clone.1 | custom fusion | flops 2097152 | bytes 25165952 | tf_op jit(solution)/shard_map/while/body/eval_jaxpr/scatter-add | solution.py:26
  72.0 4.4 gather_fusion
  76.4 7.9 %broadcast_multiply_fusion.5 = f32[32,256,256]{2,1,0:T(8,128)} fusion(f32[32]{0:T(128)S(1)} %fusion.42, bf16[32,256,256]{2,1,0:T(8,128)(2,1)} %gather_fusion, bf16[3,32,256,256]{3,2,1,0:T(8,128)(2,1)} %get-tuple-element.236, s32[]{:T(128)} %get-tuple-element.225), kind=kOutput, calls=%fused_computation.6.clone.1 | convolution fusion | flops 1075838976 | bytes 16777856 | tf_op jit(solution)/shard_map/while/body/eval_jaxpr/sab,sbf->saf/dot_general | solution.py:25
  84.3 11.7 %scatter_fusion = f32[8,256,256]{2,1,0:T(8,128)S(1)} fusion(f32[8,256,256]{2,1,0:T(8,128)S(1)} %get-tuple-element.226, s32[32]{0:T(128)S(1)} %get-tuple-element.206, f32[32,256,256]{2,1,0:T(8,128)} %broadcast_multiply_fusion.5), kind=kCustom, calls=%fused_computation.2.clone.1 | custom fusion | flops 2097152 | bytes 25165952 | tf_op jit(solution)/shard_map/while/body/eval_jaxpr/scatter-add | solution.py:26
  96.1 4.4 gather_fusion
  100.5 7.9 %broadcast_multiply_fusion.5 = f32[32,256,256]{2,1,0:T(8,128)} fusion(f32[32]{0:T(128)S(1)} %fusion.42, bf16[32,256,256]{2,1,0:T(8,128)(2,1)} %gather_fusion, bf16[3,32,256,256]{3,2,1,0:T(8,128)(2,1)} %get-tuple-element.236, s32[]{:T(128)} %get-tuple-element.225), kind=kOutput, calls=%fused_computation.6.clone.1 | convolution fusion | flops 1075838976 | bytes 16777856 | tf_op jit(solution)/shard_map/while/body/eval_jaxpr/sab,sbf->saf/dot_general | solution.py:25
  108.4 11.7 %scatter_fusion = f32[8,256,256]{2,1,0:T(8,128)S(1)} fusion(f32[8,256,256]{2,1,0:T(8,128)S(1)} %get-tuple-element.226, s32[32]{0:T(128)S(1)} %get-tuple-element.206, f32[32,256,256]{2,1,0:T(8,128)} %broadcast_multiply_fusion.5), kind=kCustom, calls=%fused_computation.2.clone.1 | custom fusion | flops 2097152 | bytes 25165952 | tf_op jit(solution)/shard_map/while/body/eval_jaxpr/scatter-add | solution.py:26
  120.2 1.3 copy-done.1
  121.5 0.0 reduce-scatter.3.cloned.1.call-update
  121.6 0.0 all-gather.5.cloned.1.call-start
  121.6 75.0 %reduce-scatter.3.cloned.1.call-done = f32[256,256]{1,0:T(8,128)} async-done(((f32[2048,256]{1,0:T(8,128)}), f32[256,256]{1,0:T(8,128)}) %reduce-scatter.3.cloned.1.call-update) | async-done | bytes 262160 | tf_op jit(solution)/shard_map/reduce_scatter | solution.py:54
  196.6 1.8 multiply_convert_fusion
  198.4 0.0 all-gather.5.cloned.1.call-update
  198.4 0.0 reduce-scatter.5.cloned.1.call-start
  198.5 16.6 %copy.10 = bf16[96,256,256]{1,2,0:T(8,128)(2,1)} copy(bf16[96,256,256]{2,1,0:T(8,128)(2,1)} %bitcast.87) | data formatting | bytes 25165824 | tf_op args[2]
  215.1 30.2 %all-gather.5.cloned.1.call-done = bf16[2048,256]{1,0:T(8,128)(2,1)} async-done(((bf16[256,256]{1,0:T(8,128)(2,1)}), bf16[2048,256]{1,0:T(8,128)(2,1)}) %all-gather.5.cloned.1.call-update) | async-done | bytes 1048592 | tf_op jit(solution)/shard_map/all_gather | solution.py:57
  245.3 2.4 broadcast_in_dim.8
  247.7 87.2 %while.21 = (s32[]{:T(128)}, f32[16,256,256]{2,1,0:T(8,128)}, s32[3,32]{1,0:T(4,128)S(1)}, bf16[3,32,256,256]{2,3,1,0:T(8,128)(2,1)}, s32[3,32]{1,0:T(4,128)S(1)...) while((s32[]{:T(128)}, f32[16,256,256]{2,1,0:T(8,128)}, s32[3,32]{1,0:T(4,128)S(1)}, ...), condition=%wide.region_6.7_spmd, body=%wide.region_4.6_spmd.sunk | while | flops 1077937408 | bytes 50337628 | solution.py:34
  247.7 2.8 gather_fusion.1
  250.5 7.9 %broadcast_multiply_fusion.6 = f32[32,256,256]{2,1,0:T(8,128)} fusion(f32[32]{0:T(128)S(1)} %fusion.46, bf16[32,256,256]{2,1,0:T(8,128)(2,1)} %gather_fusion.1, bf16[3,32,256,256]{2,3,1,0:T(8,128)(2,1)} %get-tuple-element.260, s32[]{:T(128)} %get-tuple-element.249), kind=kOutput, calls=%fused_computation.22.clone.1 | convolution fusion | flops 1075838976 | bytes 16777856 | tf_op jit(solution)/shard_map/while/body/eval_jaxpr/sab,saf->sbf/dot_general | solution.py:23
  258.4 18.5 %scatter_fusion.1 = f32[16,256,256]{2,1,0:T(8,128)} fusion(f32[16,256,256]{2,1,0:T(8,128)} %get-tuple-element.250, s32[32]{0:T(128)S(1)} %get-tuple-element.215, f32[32,256,256]{2,1,0:T(8,128)} %broadcast_multiply_fusion.6), kind=kCustom, calls=%fused_computation.3.clone.1 | custom fusion | flops 2097152 | bytes 25165952 | tf_op jit(solution)/shard_map/while/body/eval_jaxpr/scatter-add | solution.py:26
  277.0 2.8 gather_fusion.1
  279.8 7.9 %broadcast_multiply_fusion.6 = f32[32,256,256]{2,1,0:T(8,128)} fusion(f32[32]{0:T(128)S(1)} %fusion.46, bf16[32,256,256]{2,1,0:T(8,128)(2,1)} %gather_fusion.1, bf16[3,32,256,256]{2,3,1,0:T(8,128)(2,1)} %get-tuple-element.260, s32[]{:T(128)} %get-tuple-element.249), kind=kOutput, calls=%fused_computation.22.clone.1 | convolution fusion | flops 1075838976 | bytes 16777856 | tf_op jit(solution)/shard_map/while/body/eval_jaxpr/sab,saf->sbf/dot_general | solution.py:23
  287.7 18.3 %scatter_fusion.1 = f32[16,256,256]{2,1,0:T(8,128)} fusion(f32[16,256,256]{2,1,0:T(8,128)} %get-tuple-element.250, s32[32]{0:T(128)S(1)} %get-tuple-element.215, f32[32,256,256]{2,1,0:T(8,128)} %broadcast_multiply_fusion.6), kind=kCustom, calls=%fused_computation.3.clone.1 | custom fusion | flops 2097152 | bytes 25165952 | tf_op jit(solution)/shard_map/while/body/eval_jaxpr/scatter-add | solution.py:26
  306.0 2.8 gather_fusion.1
  308.8 7.9 %broadcast_multiply_fusion.6 = f32[32,256,256]{2,1,0:T(8,128)} fusion(f32[32]{0:T(128)S(1)} %fusion.46, bf16[32,256,256]{2,1,0:T(8,128)(2,1)} %gather_fusion.1, bf16[3,32,256,256]{2,3,1,0:T(8,128)(2,1)} %get-tuple-element.260, s32[]{:T(128)} %get-tuple-element.249), kind=kOutput, calls=%fused_computation.22.clone.1 | convolution fusion | flops 1075838976 | bytes 16777856 | tf_op jit(solution)/shard_map/while/body/eval_jaxpr/sab,saf->sbf/dot_general | solution.py:23
  316.7 18.2 %scatter_fusion.1 = f32[16,256,256]{2,1,0:T(8,128)} fusion(f32[16,256,256]{2,1,0:T(8,128)} %get-tuple-element.250, s32[32]{0:T(128)S(1)} %get-tuple-element.215, f32[32,256,256]{2,1,0:T(8,128)} %broadcast_multiply_fusion.6), kind=kCustom, calls=%fused_computation.3.clone.1 | custom fusion | flops 2097152 | bytes 25165952 | tf_op jit(solution)/shard_map/while/body/eval_jaxpr/scatter-add | solution.py:26
  334.9 0.0 reduce-scatter.5.cloned.1.call-update
  335.0 0.0 all-reduce.2.cloned.1.call-start
  335.0 64.2 %reduce-scatter.5.cloned.1.call-done = f32[256,256]{1,0:T(8,128)} async-done(((f32[4096,256]{1,0:T(8,128)}), f32[256,256]{1,0:T(8,128)}) %reduce-scatter.5.cloned.1.call-update) | async-done | bytes 262160 | tf_op jit(solution)/shard_map/reduce_scatter | solution.py:60
  399.2 1.8 convolution_bitcast_fusion
  401.1 0.0 all-reduce.2.cloned.1.call-update
  401.1 1.8 convolution_convert_fusion.1
  402.9 145.9 %all-reduce.2.cloned.1.call-done = f32[128,256]{0,1:T(8,128)} async-done(((f32[128,256]{0,1:T(8,128)}), f32[128,256]{0,1:T(8,128)}) %all-reduce.2.cloned.1.call-update) | async-done | bytes 131088 | tf_op jit(solution)/shard_map/psum | solution.py:69
  548.8 0.9 broadcast_multiply_fusion.2
  549.7 0.8 copy.12
  (27 shorter events, 0.2 us)
Async XLA Ops:
  7.2 0.8 copy-start
  7.2 40.4 %all-gather.3.cloned.1.call-start = ((), (), s32[]{:S(2)}) async-start(), calls=%async_computation.2 | async-start | bytes 2228224 | tf_op jit(solution)/shard_map/all_gather | solution.py:49
  9.7 186.9 %reduce-scatter.3.cloned.1.call-start = ((), (), s32[]{:S(2)}) async-start(), calls=%async_computation.3 | async-start | bytes 2359296 | tf_op jit(solution)/shard_map/reduce_scatter | solution.py:54
  47.8 148.9 %copy-start.4 = (bf16[256,256]{1,0:T(8,128)(2,1)S(1)}, bf16[256,256]{1,0:T(8,128)(2,1)}, u32[]{:S(2)}) copy-start(bf16[256,256]{1,0:T(8,128)(2,1)} %param.17) | copy-start | bytes 393220
  120.2 1.3 copy-start.1
  121.6 123.7 %all-gather.5.cloned.1.call-start = ((), (), s32[]{:S(2)}) async-start(), calls=%async_computation.4 | async-start | bytes 1179648 | tf_op jit(solution)/shard_map/all_gather | solution.py:57
  198.4 200.8 %reduce-scatter.5.cloned.1.call-start = ((), (), s32[]{:S(2)}) async-start(), calls=%async_computation.5 | async-start | bytes 4456448 | tf_op jit(solution)/shard_map/reduce_scatter | solution.py:60
  245.3 2.4 copy-start.2
  334.9 66.1 %copy-start.3 = (bf16[128,256]{1,0:T(8,128)(2,1)S(1)}, bf16[128,256]{1,0:T(8,128)(2,1)}, u32[]{:S(2)}) copy-start(bf16[128,256]{1,0:T(8,128)(2,1)} %param.12) | copy-start | bytes 196612
  335.0 213.8 %all-reduce.2.cloned.1.call-start = ((), (), s32[]{:S(2)}) async-start(), calls=%async_computation.6 | async-start | bytes 262144 | tf_op jit(solution)/shard_map/psum | solution.py:69
Sparse Core Ops, SparseCore 0:
  10.3 37.2 all-gather.2
  121.7 74.9 reduce-scatter.2
  199.6 45.6 all-gather.4
  335.1 64.0 reduce-scatter.4
  404.4 144.3 all-reduce.1
where the time goes:
time: 558 us; the launch traced here: 557 us
  waiting for transfers between devices  351 us (63%)
  other arithmetic  93.1 us (17%)
  matrix products  52.9 us (9%)
  local copies, waits for them, and re-layouts  45.1 us (8%)
  between operations  14.5 us (3%)
    psum x1, waiting for transfers between devices, body(): grad_weight = lax.psum(local_term, ('row', 'col')) / math.sqrt(nodes)  146 us
    scatter-add x6, other arithmetic, step(): return (total.at[placed].add(product * weights[:, None, None]), None)  90.3 us
    reduce_scatter x1, waiting for transfers between devices, body(): lax.psum_scatter(partial_value, 'col', scatter_dimension=0, tiled=True)  75 us
    reduce_scatter x1, waiting for transfers between devices, body(): lax.psum_scatter(back, 'row', scatter_dimension=0, tiled=True)  64.2 us
    all_gather x1, waiting for transfers between devices, body(): column_rows = lax.all_gather(projected, 'row', axis=0, tiled=True)  35.7 us
    all_gather x1, waiting for transfers between devices, body(): grad_range = lax.all_gather(grad_summed, 'col', axis=0, tiled=True)  30.2 us
    dot_general x3, matrix products, step(): jnp.einsum('sab,sbf->saf', values, picked, preferred_element_type=jnp.flo...  23.8 us
    dot_general x3, matrix products, step(): jnp.einsum('sab,saf->sbf', values, picked, preferred_element_type=jnp.flo...  23.8 us
  transfers between devices with their start and end apart: 5, of which 5 were waited for; matrix products, arithmetic and copies ran while one was open for 4% of the time, Pallas kernels for 0%

commit v1 on v0

--- a/solution.py
+++ b/solution.py
@@ -54,7 +54,11 @@
     summed = lax.psum_scatter(partial_value, "col", scatter_dimension=0, tiled=True)
     output = jax.nn.silu(summed).astype(jnp.bfloat16)
     grad_summed = (cotangent.astype(jnp.float32) * silu_slope(summed)).astype(jnp.bfloat16)
-    grad_range = lax.all_gather(grad_summed, "col", axis=0, tiled=True)
+    node_connect = lambda vector: jnp.concatenate(
+        lax.all_to_all(jnp.stack([vector for _ in range(lax.axis_size("col"))]), "col", 0, 0),
+        axis=0,
+    )
+    grad_range = node_connect(grad_summed)
     grad_blocks = grad_range.reshape(tile_rows, size, width)
     back = block_product(adj_values, slot_rows, slot_cols, keep, grad_blocks, tile_cols, True)
     grad_projected = lax.psum_scatter(back, "row", scatter_dimension=0, tiled=True).astype(

time: 558 us -> 536 us (0.961)
  waiting for transfers between devices: 351 us -> 324 us
    all_gather x1 -> x0, waiting for transfers between devices: 30.2 us -> none  [body(): grad_range = lax.all_gather(grad_summed, 'col', axis=0, tiled=True)]
    unnamed x12 -> x10, local copies, waits for them, and re-layouts: 19.5 us -> 19.5 us
  transfers between devices with their start and end apart: 5 -> 5, of which waited for: 5 -> 4; matrix products, arithmetic and copies ran while one was open for 4% -> 4% of each run, Pallas kernels for 0% -> 0%
where the time goes in v1:
time: 536 us; the launch traced here: 535 us
  waiting for transfers between devices  324 us (60%)
  other arithmetic  93 us (17%)
  matrix products  52.9 us (10%)
  local copies, waits for them, and re-layouts  46.2 us (9%)
  between operations  14.5 us (3%)
    psum x1, waiting for transfers between devices, body(): grad_weight = lax.psum(local_term, ('row', 'col')) / math.sqrt(nodes)  146 us
    scatter-add x6, other arithmetic, step(): return (total.at[placed].add(product * weights[:, None, None]), None)  90.2 us
    reduce_scatter x1, waiting for transfers between devices, body(): lax.psum_scatter(partial_value, 'col', scatter_dimension=0, tiled=True)  75.1 us
    reduce_scatter x1, waiting for transfers between devices, body(): lax.psum_scatter(back, 'row', scatter_dimension=0, tiled=True)  67.6 us
    all_gather x1, waiting for transfers between devices, body(): column_rows = lax.all_gather(projected, 'row', axis=0, tiled=True)  35.7 us
    dot_general x3, matrix products, step(): jnp.einsum('sab,sbf->saf', values, picked, preferred_element_type=jnp.flo...  23.9 us
    dot_general x3, matrix products, step(): jnp.einsum('sab,saf->sbf', values, picked, preferred_element_type=jnp.flo...  23.8 us
    gather x6, local copies, waits for them, and re-layouts, step(): picked = source[taken]  21.5 us
  transfers between devices with their start and end apart: 5, of which 4 were waited for; matrix products, arithmetic and copies ran while one was open for 4% of the time, Pallas kernels for 0%

profile of v1, /device:TPU:1, one launch (start us, length us, event | category | flops | bytes accessed | tf_op | source)
XLA Modules:
  0.0 534.8 jit_solution(15482427791717770959)
XLA Ops:
  7.2 0.0 copy-start
  7.2 0.0 all-gather.2.cloned.1.call-start
  7.2 0.8 copy-done
  8.0 1.7 convolution_convert_fusion
  9.7 0.0 all-gather.2.cloned.1.call-update
  9.7 0.0 reduce-scatter.3.cloned.1.call-start
  10.4 0.7 reshape.148
  11.1 0.7 reshape.150
  11.9 35.7 %all-gather.2.cloned.1.call-done = bf16[4096,256]{1,0:T(8,128)(2,1)} async-done(((bf16[256,256]{1,0:T(8,128)(2,1)}), bf16[4096,256]{1,0:T(8,128)(2,1)}) %all-gather.2.cloned.1.call-update) | async-done | bytes 2097168 | tf_op jit(solution)/shard_map/all_gather | solution.py:49
  47.6 0.2 broadcast_in_dim.4
  47.8 72.4 %while.20 = (s32[]{:T(128)}, f32[8,256,256]{2,1,0:T(8,128)S(1)}, s32[3,32]{1,0:T(4,128)S(1)}, bf16[3,32,256,256]{3,2,1,0:T(8,128)(2,1)}, s32[3,32]{1,0:T(4,128)S...) while((s32[]{:T(128)}, f32[8,256,256]{2,1,0:T(8,128)S(1)}, s32[3,32]{1,0:T(4,128)S(1)}, ...), condition=%wide.region_2.3_spmd, body=%wide.region_0.2_spmd.sunk | while | flops 1077937408 | bytes 50337628 | solution.py:34
  47.8 4.4 gather_fusion
  52.2 8.0 %broadcast_multiply_fusion.5 = f32[32,256,256]{2,1,0:T(8,128)} fusion(f32[32]{0:T(128)S(1)} %fusion.42, bf16[32,256,256]{2,1,0:T(8,128)(2,1)} %gather_fusion, bf16[3,32,256,256]{3,2,1,0:T(8,128)(2,1)} %get-tuple-element.236, s32[]{:T(128)} %get-tuple-element.225), kind=kOutput, calls=%fused_computation.6.clone.1 | convolution fusion | flops 1075838976 | bytes 16777856 | tf_op jit(solution)/shard_map/while/body/eval_jaxpr/sab,sbf->saf/dot_general | solution.py:25
  60.2 11.8 %scatter_fusion = f32[8,256,256]{2,1,0:T(8,128)S(1)} fusion(f32[8,256,256]{2,1,0:T(8,128)S(1)} %get-tuple-element.226, s32[32]{0:T(128)S(1)} %get-tuple-element.206, f32[32,256,256]{2,1,0:T(8,128)} %broadcast_multiply_fusion.5), kind=kCustom, calls=%fused_computation.2.clone.1 | custom fusion | flops 2097152 | bytes 25165952 | tf_op jit(solution)/shard_map/while/body/eval_jaxpr/scatter-add | solution.py:26
  72.0 4.4 gather_fusion
  76.4 8.0 %broadcast_multiply_fusion.5 = f32[32,256,256]{2,1,0:T(8,128)} fusion(f32[32]{0:T(128)S(1)} %fusion.42, bf16[32,256,256]{2,1,0:T(8,128)(2,1)} %gather_fusion, bf16[3,32,256,256]{3,2,1,0:T(8,128)(2,1)} %get-tuple-element.236, s32[]{:T(128)} %get-tuple-element.225), kind=kOutput, calls=%fused_computation.6.clone.1 | convolution fusion | flops 1075838976 | bytes 16777856 | tf_op jit(solution)/shard_map/while/body/eval_jaxpr/sab,sbf->saf/dot_general | solution.py:25
  84.3 11.7 %scatter_fusion = f32[8,256,256]{2,1,0:T(8,128)S(1)} fusion(f32[8,256,256]{2,1,0:T(8,128)S(1)} %get-tuple-element.226, s32[32]{0:T(128)S(1)} %get-tuple-element.206, f32[32,256,256]{2,1,0:T(8,128)} %broadcast_multiply_fusion.5), kind=kCustom, calls=%fused_computation.2.clone.1 | custom fusion | flops 2097152 | bytes 25165952 | tf_op jit(solution)/shard_map/while/body/eval_jaxpr/scatter-add | solution.py:26
  96.1 4.4 gather_fusion
  100.5 8.0 %broadcast_multiply_fusion.5 = f32[32,256,256]{2,1,0:T(8,128)} fusion(f32[32]{0:T(128)S(1)} %fusion.42, bf16[32,256,256]{2,1,0:T(8,128)(2,1)} %gather_fusion, bf16[3,32,256,256]{3,2,1,0:T(8,128)(2,1)} %get-tuple-element.236, s32[]{:T(128)} %get-tuple-element.225), kind=kOutput, calls=%fused_computation.6.clone.1 | convolution fusion | flops 1075838976 | bytes 16777856 | tf_op jit(solution)/shard_map/while/body/eval_jaxpr/sab,sbf->saf/dot_general | solution.py:25
  108.5 11.7 %scatter_fusion = f32[8,256,256]{2,1,0:T(8,128)S(1)} fusion(f32[8,256,256]{2,1,0:T(8,128)S(1)} %get-tuple-element.226, s32[32]{0:T(128)S(1)} %get-tuple-element.206, f32[32,256,256]{2,1,0:T(8,128)} %broadcast_multiply_fusion.5), kind=kCustom, calls=%fused_computation.2.clone.1 | custom fusion | flops 2097152 | bytes 25165952 | tf_op jit(solution)/shard_map/while/body/eval_jaxpr/scatter-add | solution.py:26
  120.2 1.3 copy-done.1
  121.6 0.0 reduce-scatter.3.cloned.1.call-update
  121.6 75.1 %reduce-scatter.3.cloned.1.call-done = f32[256,256]{1,0:T(8,128)} async-done(((f32[2048,256]{1,0:T(8,128)}), f32[256,256]{1,0:T(8,128)}) %reduce-scatter.3.cloned.1.call-update) | async-done | bytes 262160 | tf_op jit(solution)/shard_map/reduce_scatter | solution.py:54
  196.7 1.7 multiply_convert_fusion
  198.4 1.1 stack.2
  199.5 3.6 all-to-all-start
  203.1 0.0 reduce-scatter.5.cloned.1.call-start
  203.1 16.6 %copy.10 = bf16[96,256,256]{1,2,0:T(8,128)(2,1)} copy(bf16[96,256,256]{2,1,0:T(8,128)(2,1)} %bitcast.85) | data formatting | bytes 25165824 | tf_op args[2]
  219.7 2.4 broadcast_in_dim.8
  222.1 87.2 %while.21 = (s32[]{:T(128)}, f32[16,256,256]{2,1,0:T(8,128)}, s32[3,32]{1,0:T(4,128)S(1)}, bf16[3,32,256,256]{2,3,1,0:T(8,128)(2,1)}, s32[3,32]{1,0:T(4,128)S(1)...) while((s32[]{:T(128)}, f32[16,256,256]{2,1,0:T(8,128)}, s32[3,32]{1,0:T(4,128)S(1)}, ...), condition=%wide.region_6.7_spmd, body=%wide.region_4.6_spmd.sunk | while | flops 1077937408 | bytes 50337628 | solution.py:34
  222.2 2.8 gather_fusion.1
  224.9 7.9 %broadcast_multiply_fusion.6 = f32[32,256,256]{2,1,0:T(8,128)} fusion(f32[32]{0:T(128)S(1)} %fusion.46, bf16[32,256,256]{2,1,0:T(8,128)(2,1)} %gather_fusion.1, bf16[3,32,256,256]{2,3,1,0:T(8,128)(2,1)} %get-tuple-element.260, s32[]{:T(128)} %get-tuple-element.249), kind=kOutput, calls=%fused_computation.22.clone.1 | convolution fusion | flops 1075838976 | bytes 16777856 | tf_op jit(solution)/shard_map/while/body/eval_jaxpr/sab,saf->sbf/dot_general | solution.py:23
  232.9 18.4 %scatter_fusion.1 = f32[16,256,256]{2,1,0:T(8,128)} fusion(f32[16,256,256]{2,1,0:T(8,128)} %get-tuple-element.250, s32[32]{0:T(128)S(1)} %get-tuple-element.215, f32[32,256,256]{2,1,0:T(8,128)} %broadcast_multiply_fusion.6), kind=kCustom, calls=%fused_computation.3.clone.1 | custom fusion | flops 2097152 | bytes 25165952 | tf_op jit(solution)/shard_map/while/body/eval_jaxpr/scatter-add | solution.py:26
  251.3 2.8 gather_fusion.1
  254.1 7.9 %broadcast_multiply_fusion.6 = f32[32,256,256]{2,1,0:T(8,128)} fusion(f32[32]{0:T(128)S(1)} %fusion.46, bf16[32,256,256]{2,1,0:T(8,128)(2,1)} %gather_fusion.1, bf16[3,32,256,256]{2,3,1,0:T(8,128)(2,1)} %get-tuple-element.260, s32[]{:T(128)} %get-tuple-element.249), kind=kOutput, calls=%fused_computation.22.clone.1 | convolution fusion | flops 1075838976 | bytes 16777856 | tf_op jit(solution)/shard_map/while/body/eval_jaxpr/sab,saf->sbf/dot_general | solution.py:23
  262.1 18.3 %scatter_fusion.1 = f32[16,256,256]{2,1,0:T(8,128)} fusion(f32[16,256,256]{2,1,0:T(8,128)} %get-tuple-element.250, s32[32]{0:T(128)S(1)} %get-tuple-element.215, f32[32,256,256]{2,1,0:T(8,128)} %broadcast_multiply_fusion.6), kind=kCustom, calls=%fused_computation.3.clone.1 | custom fusion | flops 2097152 | bytes 25165952 | tf_op jit(solution)/shard_map/while/body/eval_jaxpr/scatter-add | solution.py:26
  280.4 2.8 gather_fusion.1
  283.2 7.9 %broadcast_multiply_fusion.6 = f32[32,256,256]{2,1,0:T(8,128)} fusion(f32[32]{0:T(128)S(1)} %fusion.46, bf16[32,256,256]{2,1,0:T(8,128)(2,1)} %gather_fusion.1, bf16[3,32,256,256]{2,3,1,0:T(8,128)(2,1)} %get-tuple-element.260, s32[]{:T(128)} %get-tuple-element.249), kind=kOutput, calls=%fused_computation.22.clone.1 | convolution fusion | flops 1075838976 | bytes 16777856 | tf_op jit(solution)/shard_map/while/body/eval_jaxpr/sab,saf->sbf/dot_general | solution.py:23
  291.1 18.2 %scatter_fusion.1 = f32[16,256,256]{2,1,0:T(8,128)} fusion(f32[16,256,256]{2,1,0:T(8,128)} %get-tuple-element.250, s32[32]{0:T(128)S(1)} %get-tuple-element.215, f32[32,256,256]{2,1,0:T(8,128)} %broadcast_multiply_fusion.6), kind=kCustom, calls=%fused_computation.3.clone.1 | custom fusion | flops 2097152 | bytes 25165952 | tf_op jit(solution)/shard_map/while/body/eval_jaxpr/scatter-add | solution.py:26
  309.4 0.0 reduce-scatter.5.cloned.1.call-update
  309.4 0.0 all-reduce.2.cloned.1.call-start
  309.4 67.6 %reduce-scatter.5.cloned.1.call-done = f32[256,256]{1,0:T(8,128)} async-done(((f32[4096,256]{1,0:T(8,128)}), f32[256,256]{1,0:T(8,128)}) %reduce-scatter.5.cloned.1.call-update) | async-done | bytes 262160 | tf_op jit(solution)/shard_map/reduce_scatter | solution.py:64
  377.1 1.8 convolution_bitcast_fusion
  378.9 0.0 all-reduce.2.cloned.1.call-update
  378.9 1.8 convolution_convert_fusion.1
  380.7 145.9 %all-reduce.2.cloned.1.call-done = f32[128,256]{0,1:T(8,128)} async-done(((f32[128,256]{0,1:T(8,128)}), f32[128,256]{0,1:T(8,128)}) %all-reduce.2.cloned.1.call-update) | async-done | bytes 131088 | tf_op jit(solution)/shard_map/psum | solution.py:73
  526.6 0.9 broadcast_multiply_fusion.2
  527.5 0.8 copy.12
  (25 shorter events, 0.1 us)
Async XLA Ops:
  7.2 0.8 copy-start
  7.2 40.4 %all-gather.2.cloned.1.call-start = ((), (), s32[]{:S(2)}) async-start(), calls=%async_computation.3 | async-start | bytes 2228224 | tf_op jit(solution)/shard_map/all_gather | solution.py:49
  9.7 187.0 %reduce-scatter.3.cloned.1.call-start = ((), (), s32[]{:S(2)}) async-start(), calls=%async_computation.4 | async-start | bytes 2359296 | tf_op jit(solution)/shard_map/reduce_scatter | solution.py:54
  47.8 148.9 %copy-start.3 = (bf16[256,256]{1,0:T(8,128)(2,1)S(1)}, bf16[256,256]{1,0:T(8,128)(2,1)}, u32[]{:S(2)}) copy-start(bf16[256,256]{1,0:T(8,128)(2,1)} %param.17) | copy-start | bytes 393220
  120.2 1.3 copy-start.1
  199.5 20.2 %all-to-all-start = ((bf16[8,256,256]{2,1,0:T(8,128)(2,1)}), bf16[8,256,256]{2,1,0:T(8,128)(2,1)S(1)}, u32[]{:S(2)}, u32[]{:S(2)}) async-start(bf16[8,256,256]{2,1,0:T(8,128)(2,1)} %stack.2), calls=%async_computation.1 | async-start | bytes 2097152 | tf_op jit(solution)/shard_map/all_to_all | solution.py:58
  203.1 174.0 %reduce-scatter.5.cloned.1.call-start = ((), (), s32[]{:S(2)}) async-start(), calls=%async_computation.5 | async-start | bytes 4456448 | tf_op jit(solution)/shard_map/reduce_scatter | solution.py:64
  309.4 69.6 %copy-start.2 = (bf16[128,256]{1,0:T(8,128)(2,1)S(1)}, bf16[128,256]{1,0:T(8,128)(2,1)}, u32[]{:S(2)}) copy-start(bf16[128,256]{1,0:T(8,128)(2,1)} %param.12) | copy-start | bytes 196612
  309.4 217.2 %all-reduce.2.cloned.1.call-start = ((), (), s32[]{:S(2)}) async-start(), calls=%async_computation.6 | async-start | bytes 262144 | tf_op jit(solution)/shard_map/psum | solution.py:73
Sparse Core Ops, SparseCore 0:
  10.3 37.2 all-gather.1
  121.7 74.9 reduce-scatter.2
  309.5 67.5 reduce-scatter.4
  382.2 144.3 all-reduce.1
